TPU v7x, 32 devices: a whole 2x2x4 slice. The times are simulated.
32 devices in a mesh: dp: 8 (over z, x), seq: 4 (over y, core).
Axes of the slice: x: 2, y: 2, z: 4, core: 2. Of those that a mesh axis runs over, the one named last changes fastest.
Arguments:
- tokens: bfloat16 [16384, 1024], P(('dp', 'seq')), may hold values from -6 to 6
- time_embed: bfloat16 [32, 1024], P(('dp', 'seq')), may hold values from -6 to 6
- lengths: int32 [32], P('dp'), may hold values from 0 to 475, as said below
- cotangent: bfloat16 [16384, 1024], P(('dp', 'seq')), may hold values from -6 to 6
- w_query: bfloat16 [1024, 1024], P('seq'), may hold values from -0.1875 to 0.1875
- w_key: bfloat16 [1024, 1024], P('seq'), may hold values from -0.1875 to 0.1875
- w_value: bfloat16 [1024, 1024], P('seq'), may hold values from -0.1875 to 0.1875
- w_out: bfloat16 [1024, 1024], P('seq'), may hold values from -0.75 to 0.75
- w_time: bfloat16 [1024, 1024], P('seq'), may hold values from -0.1875 to 0.1875
- w_in: bfloat16 [4096, 1024], P('seq'), may hold values from -0.1875 to 0.1875
- w_down: bfloat16 [4096, 1024], P('seq'), may hold values from -0.09375 to 0.09375
- b_query: bfloat16 [1024], replicated, may hold values from -3 to 3
- b_value: bfloat16 [1024], replicated, may hold values from -3 to 3
- b_out: bfloat16 [1024], replicated, may hold values from -3 to 3
- b_time: bfloat16 [1024], replicated, may hold values from -3 to 3
- b_in: bfloat16 [4096], replicated, may hold values from -3 to 3
- b_down: bfloat16 [1024], replicated, may hold values from -2 to 2
- gain_one: bfloat16 [1024], replicated, may hold values from 0.25 to 1.75
- shift_one: bfloat16 [1024], replicated, may hold values from -2 to 2
- gain_two: bfloat16 [1024], replicated, may hold values from 0.25 to 1.75
- shift_two: bfloat16 [1024], replicated, may hold values from -2 to 2
Outputs:
- layer_out: bfloat16 [16384, 1024], P(('dp', 'seq'))
- grad_tokens: bfloat16 [16384, 1024], P(('dp', 'seq'))
- grad_w_query: float32 [1024, 1024], P('seq')
- grad_w_key: float32 [1024, 1024], P('seq')
- grad_w_value: float32 [1024, 1024], P('seq')
- grad_w_out: float32 [1024, 1024], P('seq')
- grad_w_time: float32 [1024, 1024], P('seq')
- grad_w_in: float32 [4096, 1024], P('seq')
- grad_w_down: float32 [4096, 1024], P('seq')
- grad_b_query: float32 [1024], replicated
- grad_b_value: float32 [1024], replicated
- grad_b_out: float32 [1024], replicated
- grad_b_time: float32 [1024], replicated
- grad_b_in: float32 [4096], replicated
- grad_b_down: float32 [1024], replicated
- grad_gain_one: float32 [1024], replicated
- grad_shift_one: float32 [1024], replicated
- grad_gain_two: float32 [1024], replicated
- grad_shift_two: float32 [1024], replicated
Inputs may be any that keep to these rules, and one draw needn't show every extreme that they name: Item i's valid slots are its first lengths[i] + 25; every draw has an item of length 475 and one of length 0.
All inputs are finite; a program needn't handle non-finite values.
Results may differ from a plain program's by a relative error of at most 0.02.
Values may be sent and summed in bfloat16 or wider, within the bound.
A program may use at most 256 MiB of HBM per device.

v0:
```python
import jax
import jax.numpy as jnp
from jax import lax
from jax.sharding import PartitionSpec as P

HEAD_DIM = 64
BLOCK = 25
norm_eps = 1e-05
neg_large = -1e30


def layer_norm(values, gain, shift):
    center = values - jnp.mean(values, axis=-1, keepdims=True)
    spread = lax.rsqrt(jnp.mean(center * center, axis=-1, keepdims=True) + norm_eps)
    return center * spread * gain + shift


def exact_gelu(values):
    return jax.nn.gelu(values, approximate=False)


def split_heads(rows):
    return rows.reshape(rows.shape[0], rows.shape[1] // HEAD_DIM, HEAD_DIM)


def item_scores(queries, keys, key_valid):
    scores = jnp.einsum(
        "qhd,khd->hqk", split_heads(queries), split_heads(keys), preferred_element_type=jnp.float32
    ) * HEAD_DIM ** (-0.5)
    return jnp.where(key_valid[None, None, :], scores, neg_large)


def attend_forward(queries, keys, values, key_valid):
    masked = item_scores(queries, keys, key_valid)
    row_max = jnp.max(masked, axis=-1, keepdims=True)
    exp_scores = jnp.exp(masked - row_max)
    row_total = jnp.sum(exp_scores, axis=-1, keepdims=True)
    soft = (exp_scores / row_total).astype(jnp.bfloat16)
    mixed = jnp.einsum(
        "hqk,khd->qhd", soft, split_heads(values), preferred_element_type=jnp.float32
    )
    log_total = row_max[:, :, 0] + jnp.log(row_total[:, :, 0])
    return (mixed.reshape(queries.shape).astype(jnp.bfloat16), log_total)


def attend_backward(queries, keys, values, key_valid, log_total, grad_mixed):
    masked = item_scores(queries, keys, key_valid)
    soft = jnp.exp(masked - log_total[:, :, None])
    grad_heads = split_heads(grad_mixed)
    grad_value = jnp.einsum(
        "hqk,qhd->khd", soft.astype(jnp.bfloat16), grad_heads, preferred_element_type=jnp.float32
    )
    grad_soft = jnp.einsum(
        "qhd,khd->hqk", grad_heads, split_heads(values), preferred_element_type=jnp.float32
    )
    grad_scores = soft * (grad_soft - jnp.sum(soft * grad_soft, axis=-1, keepdims=True))
    scores_low = grad_scores.astype(jnp.bfloat16)
    scale = HEAD_DIM ** (-0.5)
    grad_query = scale * jnp.einsum(
        "hqk,khd->qhd", scores_low, split_heads(keys), preferred_element_type=jnp.float32
    )
    grad_key = scale * jnp.einsum(
        "hqk,qhd->khd", scores_low, split_heads(queries), preferred_element_type=jnp.float32
    )
    return tuple(
        (
            grad.reshape(queries.shape).astype(jnp.bfloat16)
            for grad in (grad_query, grad_key, grad_value)
        )
    )


def per_item(fn, item_count, slot_count, *arrays):
    if item_count == 1:
        return fn(*[a[0] for a in arrays])
    outs = lax.map(lambda packed: fn(*packed), arrays)
    return outs


def local(
    tokens,
    time_embed,
    lengths,
    cotangent,
    w_query,
    w_key,
    w_value,
    w_out,
    w_time,
    w_in,
    w_down,
    b_query,
    b_value,
    b_out,
    b_time,
    b_in,
    b_down,
    gain_one,
    shift_one,
    gain_two,
    shift_two,
):
    f32, bf16 = (jnp.float32, jnp.bfloat16)
    seq_rank = lax.axis_index("seq")
    item_count = time_embed.shape[0]
    token_count = tokens.shape[0]
    slot_count = token_count // item_count
    width = tokens.shape[1]
    rows = w_time.shape[0]

    def mm(a, b, dims):
        return lax.dot_general(a, b, (dims, ((), ())), preferred_element_type=f32)

    def gather(a):
        return lax.all_gather(a, "seq", axis=0, tiled=True)

    def scatter_sum(a):
        return lax.psum_scatter(a, "seq", scatter_dimension=0, tiled=True)

    full_time, full_query, full_key, full_value, full_out = (
        gather(w_time),
        gather(w_query),
        gather(w_key),
        gather(w_value),
        gather(w_out),
    )
    own_lengths = lax.dynamic_slice_in_dim(lengths, seq_rank * item_count, item_count, 0)
    slot_index = lax.broadcasted_iota(jnp.int32, (item_count, slot_count), 1)
    own_valid = slot_index < own_lengths[:, None] + BLOCK
    row_keep = own_valid.reshape(token_count, 1).astype(f32)
    time_proj = mm(time_embed, full_time, ((1,), (0,))) + b_time.astype(f32)
    resid = (tokens.reshape(item_count, slot_count, width) + time_proj[:, None, :]).reshape(
        token_count, width
    )
    resid_low = resid.astype(bf16)
    query_rows = (mm(resid_low, full_query, ((1,), (0,))) + b_query.astype(f32)).astype(bf16)
    key_rows = mm(resid_low, full_key, ((1,), (0,))).astype(bf16)
    value_rows = (mm(resid_low, full_value, ((1,), (0,))) + b_value.astype(f32)).astype(bf16)

    def split_items(a):
        return a.reshape(item_count, slot_count, -1)

    qkv = [split_items(a) for a in (query_rows, key_rows, value_rows)]
    mixed, log_total = per_item(attend_forward, item_count, slot_count, *qkv, own_valid)
    mixed_rows = mixed.reshape(token_count, width)
    attn_out = mm(mixed_rows, full_out, ((1,), (0,))) + b_out.astype(f32)
    first_norm, first_pull = jax.vjp(
        layer_norm, resid + attn_out, gain_one.astype(f32), shift_one.astype(f32)
    )
    first_group = gather(first_norm.astype(bf16))
    bias_in = lax.dynamic_slice_in_dim(b_in, seq_rank * w_in.shape[0], w_in.shape[0], 0)
    hidden_pre = mm(first_group, w_in, ((1,), (1,))) + bias_in.astype(f32)
    hidden, gelu_pull = jax.vjp(exact_gelu, hidden_pre)
    hidden_low = hidden.astype(bf16)
    ffn_part = mm(hidden_low, w_down, ((1,), (0,))).astype(bf16)
    ffn_out = scatter_sum(ffn_part).astype(f32) + b_down.astype(f32)
    second_norm, second_pull = jax.vjp(
        layer_norm, first_norm + ffn_out, gain_two.astype(f32), shift_two.astype(f32)
    )
    layer_out = (second_norm * row_keep).astype(bf16)
    grad_second_in, grad_gain_two, grad_shift_two = second_pull(cotangent.astype(f32) * row_keep)
    grad_ffn = grad_second_in.astype(bf16)
    grad_group = gather(grad_ffn)
    grad_hidden = mm(grad_group, w_down, ((1,), (1,)))
    grad_pre = gelu_pull(grad_hidden)[0].astype(bf16)
    back_part = mm(grad_pre, w_in, ((1,), (0,))).astype(bf16)
    grad_first = grad_second_in + scatter_sum(back_part).astype(f32)
    term_in = mm(grad_pre, first_group, ((0,), (0,))).astype(bf16)
    term_down = mm(hidden_low, grad_group, ((0,), (0,))).astype(bf16)
    sum_ffn = lax.psum(jnp.concatenate([term_in, term_down], axis=0), "dp").astype(f32)
    grad_first_in, grad_gain_one, grad_shift_one = first_pull(grad_first)
    grad_attn = grad_first_in.astype(bf16)
    grad_mixed = mm(grad_attn, full_out, ((1,), (1,))).astype(bf16)
    if item_count == 1:
        extra = (log_total[None], split_items(grad_mixed))
    else:
        extra = (log_total, split_items(grad_mixed))
    grad_query, grad_key, grad_value = (
        a.reshape(token_count, width)
        for a in per_item(attend_backward, item_count, slot_count, *qkv, own_valid, *extra)
    )
    grad_resid = (
        grad_first_in
        + mm(grad_query, full_query, ((1,), (1,)))
        + mm(grad_key, full_key, ((1,), (1,)))
        + mm(grad_value, full_value, ((1,), (1,)))
    )
    grad_tokens = grad_resid.astype(bf16)
    grad_time = jnp.sum(grad_resid.reshape(item_count, slot_count, width), axis=1).astype(bf16)
    terms = [
        mm(resid_low, grad_query, ((0,), (0,))),
        mm(resid_low, grad_key, ((0,), (0,))),
        mm(resid_low, grad_value, ((0,), (0,))),
        mm(mixed_rows, grad_attn, ((0,), (0,))),
    ]
    group = w_out.shape[0]
    stacked = jnp.stack([t.astype(bf16).reshape(-1, group, width) for t in terms], axis=1)
    share = scatter_sum(stacked.reshape(-1, width))
    sum_attn = lax.psum(share, "dp").astype(f32)
    small = jnp.concatenate(
        [
            jnp.stack(
                [
                    jnp.sum(grad_query, axis=0, dtype=f32),
                    jnp.sum(grad_value, axis=0, dtype=f32),
                    jnp.sum(grad_attn, axis=0, dtype=f32),
                    jnp.sum(grad_ffn, axis=0, dtype=f32),
                    grad_gain_one,
                    grad_shift_one,
                    grad_gain_two,
                    grad_shift_two,
                ]
            ).astype(bf16),
            jnp.sum(grad_pre, axis=0, dtype=f32).reshape(-1, width).astype(bf16),
            time_embed,
            grad_time,
        ],
        axis=0,
    )
    every = lax.all_gather(small, ("dp", "seq"), axis=0)
    vectors = jnp.sum(every[:, :8], axis=0, dtype=f32)
    hidden_rows = every.shape[1] - 8 - 2 * item_count
    in_parts = every[:, 8 : 8 + hidden_rows].reshape(-1, b_in.shape[0])
    grad_b_in = jnp.sum(in_parts, axis=0, dtype=f32)
    time_rows = every[:, 8 + hidden_rows : 8 + hidden_rows + item_count].reshape(-1, width)
    time_grads = every[:, 8 + hidden_rows + item_count :].reshape(-1, width)
    own_columns = lax.dynamic_slice_in_dim(time_rows, seq_rank * rows, rows, 1)
    grad_w_time = mm(own_columns, time_grads, ((0,), (0,)))
    grad_b_time = jnp.sum(time_grads, axis=0, dtype=f32)
    return (
        layer_out,
        grad_tokens,
        sum_attn[:group],
        sum_attn[group : 2 * group],
        sum_attn[2 * group : 3 * group],
        sum_attn[3 * group :],
        grad_w_time,
        sum_ffn[: w_in.shape[0]],
        sum_ffn[w_in.shape[0] :],
        vectors[0],
        vectors[1],
        vectors[2],
        grad_b_time,
        grad_b_in,
        vectors[3],
        vectors[4],
        vectors[5],
        vectors[6],
        vectors[7],
    )


def solution(mesh):
    in_specs = (
        P(("dp", "seq"), None),
        P(("dp", "seq"), None),
        P("dp"),
        P(("dp", "seq"), None),
        P("seq", None),
        P("seq", None),
        P("seq", None),
        P("seq", None),
        P("seq", None),
        P("seq", None),
        P("seq", None),
        P(),
        P(),
        P(),
        P(),
        P(),
        P(),
        P(),
        P(),
        P(),
        P(),
    )
    out_specs = (
        P(("dp", "seq"), None),
        P(("dp", "seq"), None),
        P("seq", None),
        P("seq", None),
        P("seq", None),
        P("seq", None),
        P("seq", None),
        P("seq", None),
        P("seq", None),
        P(),
        P(),
        P(),
        P(),
        P(),
        P(),
        P(),
        P(),
        P(),
        P(),
    )
    return jax.shard_map(local, mesh=mesh, in_specs=in_specs, out_specs=out_specs, check_vma=False)
```

profile of v0, /device:TPU:0, one launch (start us, length us, event | category | flops | bytes accessed | tf_op | source)
XLA Modules:
  0.0 732.2 jit_solution(3286179977434555433)
XLA Ops:
  16.0 18.9 %all-gather.10.cloned.1.call-done = bf16[1024,1024]{1,0:T(8,128)(2,1)} async-done(((bf16[256,1024]{1,0:T(8,128)(2,1)}), bf16[1024,1024]{1,0:T(8,128)(2,1)}) %all-gather.10.cloned.1.call-update) | async-done | bytes 2097168 | tf_op jit(solution)/shard_map/all_gather | solution.py:115
  36.9 22.1 %all-gather.14.cloned.1.call-done = bf16[1024,1024]{1,0:T(8,128)(2,1)} async-done(((bf16[256,1024]{1,0:T(8,128)(2,1)}), bf16[1024,1024]{1,0:T(8,128)(2,1)}) %all-gather.14.cloned.1.call-update) | async-done | bytes 2097168 | tf_op jit(solution)/shard_map/all_gather | solution.py:115
  63.6 19.7 %all-gather.16.cloned.1.call-done = bf16[1024,1024]{1,0:T(8,128)(2,1)} async-done(((bf16[256,1024]{1,0:T(8,128)(2,1)}), bf16[1024,1024]{1,0:T(8,128)(2,1)}) %all-gather.16.cloned.1.call-update) | async-done | bytes 2097168 | tf_op jit(solution)/shard_map/all_gather | solution.py:115
  88.9 9.2 %fusion.46 = (f32[16,512]{1,0:T(8,128)S(1)}, f32[16,512,512]{1,2,0:T(8,128)}) fusion(bf16[512,16,64]{0,2,1:T(8,128)(2,1)} %bitcast.89, bf16[512,16,64]{0,2,1:T(8,128)(2,1)S(1)} %bitcast.87, pred[512]{0:T(512)(128)(4,1)S(1)} %iota_compare_fusion), kind=kOutput, calls=%fused_computation.107 | convolution fusion | flops 549445632 | bytes 18907648 | tf_op jit(solution)/shard_map/qhd,khd->hqk/dot_general | solution.py:27
  98.0 9.2 %all-gather.12.cloned.1.call-done = bf16[1024,1024]{1,0:T(8,128)(2,1)} async-done(((bf16[256,1024]{1,0:T(8,128)(2,1)}), bf16[1024,1024]{1,0:T(8,128)(2,1)}) %all-gather.12.cloned.1.call-update) | async-done | bytes 2097168 | tf_op jit(solution)/shard_map/all_gather | solution.py:115
  112.9 9.4 %fusion = f32[16,512]{1,0:T(8,128)S(1)} fusion(f32[16,512,512]{1,2,0:T(8,128)} %get-tuple-element.61, f32[16,512]{1,0:T(8,128)S(1)} %get-tuple-element.60), kind=kLoop, calls=%fused_computation.6 | loop fusion | flops 8380416 | bytes 16842752 | tf_op jit(solution)/shard_map/reduce_sum | solution.py:37
  122.2 8.5 %fusion.16 = bf16[16,64,512]{2,1,0:T(8,128)(2,1)} fusion(bf16[512,16,64]{0,2,1:T(8,128)(2,1)S(1)} %bitcast.93, f32[16,512,512]{1,2,0:T(8,128)} %get-tuple-element.61, f32[16,512]{1,0:T(8,128)S(1)} %fusion, f32[16,512]{1,0:T(8,128)S(1)} %get-tuple-element.60), kind=kOutput, calls=%fused_computation.64 | convolution fusion | flops 549978112 | bytes 18939904 | tf_op jit(solution)/shard_map/hqk,khd->qhd/dot_general | solution.py:39
  138.5 33.7 %all-gather.20.cloned.1.call-done = bf16[2048,1024]{1,0:T(8,128)(2,1)} async-done(((bf16[512,1024]{1,0:T(8,128)(2,1)}), bf16[2048,1024]{1,0:T(8,128)(2,1)}) %all-gather.20.cloned.1.call-update) | async-done | bytes 4194320 | tf_op jit(solution)/shard_map/all_gather | solution.py:115
  172.1 25.7 %multiply_convert_fusion.1 = (bf16[2048,1024]{1,0:T(8,128)(2,1)S(1)}, f32[2048,1024]{1,0:T(8,128)}, f32[2048,1024]{1,0:T(8,128)}) fusion(f32[1024]{0:T(1024)S(1)} %dynamic-slice_convert_fusion, bf16[2048,1024]{1,0:T(8,128)(2,1)} %all-gather.20.cloned.1.call-done, bf16[1024,1024]{1,0:T(8,128)(2,1)S(1)} %copy-done), kind=kOutput, calls=%fused_computation.14 | convolution fusion | flops 4433379328 | bytes 27267072 | tf_op jit(solution)/shard_map/dot_general | solution.py:112
  199.8 6.0 convolution_convert_fusion.1
  206.6 44.0 %reduce-scatter.4.cloned.1.call-done = bf16[512,1024]{1,0:T(8,128)(2,1)} async-done(((bf16[2048,1024]{1,0:T(8,128)(2,1)}), bf16[512,1024]{1,0:T(8,128)(2,1)}) %reduce-scatter.4.cloned.1.call-update) | async-done | bytes 1048592 | tf_op jit(solution)/shard_map/reduce_scatter | solution.py:118
  259.6 34.2 %all-gather.22.cloned.1.call-done = bf16[2048,1024]{1,0:T(8,128)(2,1)} async-done(((bf16[512,1024]{1,0:T(8,128)(2,1)}), bf16[2048,1024]{1,0:T(8,128)(2,1)}) %all-gather.22.cloned.1.call-update) | async-done | bytes 4194320 | tf_op jit(solution)/shard_map/all_gather | solution.py:115
  293.8 13.3 %fusion.34 = (bf16[1024]{0:T(1024)(128)(2,1)S(1)}, bf16[2048,1024]{1,0:T(8,128)(2,1)S(1)}) fusion(f32[2048,1024]{1,0:T(8,128)} %get-tuple-element.40, f32[2048,1024]{1,0:T(8,128)} %get-tuple-element.64, f32[1024]{0:T(1024)S(1)} %dynamic-slice_convert_fusion, bf16[2048,1024]{1,0:T(8,128)(2,1)} %all-gather.22.cloned.1.call-done, bf16[1024,1024]{1,0:T(8,128)(2,1)} %param.31), kind=kOutput, calls=%fused_computation.96 | convolution fusion | flops 4328520704 | bytes 27269120 | tf_op jit(solution)/shard_map/dot_general | solution.py:112
  309.1 6.0 convolution_convert_fusion
  315.2 44.7 %reduce-scatter.6.cloned.1.call-done = bf16[512,1024]{1,0:T(8,128)(2,1)} async-done(((bf16[2048,1024]{1,0:T(8,128)(2,1)}), bf16[512,1024]{1,0:T(8,128)(2,1)}) %reduce-scatter.6.cloned.1.call-update) | async-done | bytes 1048592 | tf_op jit(solution)/shard_map/reduce_scatter | solution.py:118
  370.2 11.4 %multiply_reduce_fusion = (f32[16,512]{1,0:T(8,128)S(1)}, f32[16,512,512]{1,2,0:T(8,128)}) fusion(f32[16,512,512]{1,2,0:T(8,128)} %get-tuple-element.61, f32[16,512]{1,0:T(8,128)S(1)} %log_add_fusion, bf16[512,16,64]{0,2,1:T(8,128)(2,1)S(1)} %bitcast.91, bf16[512,16,64]{0,2,1:T(8,128)(2,1)} %bitcast.94), kind=kOutput, calls=%fused_computation.1 | convolution fusion | flops 549445632 | bytes 35717120 | tf_op jit(solution)/shard_map/qhd,khd->hqk/dot_general | solution.py:53
  381.6 12.0 %multiply_convert_fusion = bf16[16,512,512]{1,2,0:T(8,128)(2,1)S(1)} fusion(f32[16,512,512]{1,2,0:T(8,128)} %get-tuple-element.66, f32[16,512,512]{1,2,0:T(8,128)} %get-tuple-element.61, f32[16,512]{1,0:T(8,128)S(1)} %get-tuple-element.65, f32[16,512]{1,0:T(8,128)S(1)} %log_add_fusion), kind=kLoop, calls=%fused_computation | loop fusion | flops 16777216 | bytes 42008576 | tf_op jit(solution)/shard_map/convert_element_type | solution.py:57
  399.1 8.6 %bitcast_reduce_fusion = (bf16[16,64]{1,0:T(8,128)(2,1)S(1)}, bf16[16,64,512]{2,1,0:T(8,128)(2,1)S(1)}) fusion(bf16[512,16,64]{0,2,1:T(8,128)(2,1)S(1)} %bitcast.92, f32[16,512,512]{1,2,0:T(8,128)} %get-tuple-element.61, f32[16,512]{1,0:T(8,128)S(1)} %log_add_fusion), kind=kOutput, calls=%fused_computation.68 | convolution fusion | flops 546307072 | bytes 18909184 | tf_op jit(solution)/shard_map/hqk,qhd->khd/dot_general | solution.py:50
  415.6 7.9 %copy.79 = bf16[4,4,256,1024]{3,2,1,0:T(8,128)(2,1)} copy(bf16[4,4,256,1024]{3,2,0,1:T(8,128)(2,1)} %pad_maximum_fusion) | data formatting | bytes 16777216 | tf_op jit(solution)/shard_map/stack | solution.py:197
  423.9 8.2 %convolution_convert_fusion.2 = bf16[1024,1024]{1,0:T(8,128)(2,1)S(1)} fusion(bf16[2048,1024]{1,0:T(8,128)(2,1)} %copy-done.36, bf16[2048,1024]{1,0:T(8,128)(2,1)} %all-gather.22.cloned.1.call-done), kind=kOutput, calls=%fused_computation.57 | convolution fusion | flops 4296015872 | bytes 10485760 | tf_op jit(solution)/shard_map/dot_general | solution.py:112
  439.3 55.8 %reduce-scatter.8.cloned.1.call-done = bf16[1024,1024]{1,0:T(8,128)(2,1)} async-done(((bf16[4096,1024]{1,0:T(8,128)(2,1)}), bf16[1024,1024]{1,0:T(8,128)(2,1)}) %reduce-scatter.8.cloned.1.call-update) | async-done | bytes 2097168 | tf_op jit(solution)/shard_map/reduce_scatter | solution.py:118
  503.7 51.7 %all-gather.1 = bf16[32,11,1024]{2,1,0:T(8,128)(2,1)S(1)} all-gather(bf16[1,11,1024]{2,1,0:T(8,128)(2,1)S(1)} %bitcast.107), channel_id=2, replica_groups=mesh['dp'=8,'seq'=4] {'dp','seq'}, dimensions={0}, use_global_device_ids=true | all-gather | bytes 743424 | tf_op jit(solution)/shard_map/all_gather | solution.py:220
  559.3 156.8 %all-reduce.3.cloned.1.call-done = (bf16[1024,1024]{1,0:T(8,128)(2,1)}, bf16[2048,1024]{1,0:T(8,128)(2,1)}) async-done(((bf16[1024,1024]{1,0:T(8,128)(2,1)}, bf16[2048,1024]{1,0:T(8,128)(2,1)}), (bf16[1024,1024]{1,0:T(8,128)(2,1)}, bf16[2048,1024]{1,0:T(8,128)(2,1)})) %all-reduce.3.cloned.1.call-update) | async-done | bytes 6291472 | tf_op jit(solution)/shard_map/psum | solution.py:199
  716.2 6.8 fusion.41
  (176 shorter events, 92.8 us)
Async XLA Ops:
  7.2 164.9 %copy-start = (bf16[1024,1024]{1,0:T(8,128)(2,1)S(1)}, bf16[1024,1024]{1,0:T(8,128)(2,1)}, u32[]{:S(2)}) copy-start(bf16[1024,1024]{1,0:T(8,128)(2,1)} %param.30) | copy-start | bytes 6291460
  7.2 29.7 %copy-start.28 = (bf16[1024]{0:T(1024)(128)(2,1)S(1)}, bf16[1024]{0:T(1024)(128)(2,1)}, u32[]{:S(2)}) copy-start(bf16[1024]{0:T(1024)(128)(2,1)} %param.35) | copy-start | bytes 6148
  7.2 27.7 %all-gather.10.cloned.1.call-start = ((), (), s32[]{:S(2)}) async-start(), calls=%async_computation.3 | async-start | bytes 2621440 | tf_op jit(solution)/shard_map/all_gather | solution.py:115
  7.9 51.1 %all-gather.14.cloned.1.call-start = ((), (), s32[]{:S(2)}) async-start(), calls=%async_computation.5 | async-start | bytes 2621440 | tf_op jit(solution)/shard_map/all_gather | solution.py:115
  8.7 74.5 %all-gather.16.cloned.1.call-start = ((), (), s32[]{:S(2)}) async-start(), calls=%async_computation.6 | async-start | bytes 2621440 | tf_op jit(solution)/shard_map/all_gather | solution.py:115
  9.4 97.8 %all-gather.12.cloned.1.call-start = ((), (), s32[]{:S(2)}) async-start(), calls=%async_computation.4 | async-start | bytes 2621440 | tf_op jit(solution)/shard_map/all_gather | solution.py:115
  10.0 121.2 %all-gather.18.cloned.1.call-start = ((), (), s32[]{:S(2)}) async-start(), calls=%async_computation.7 | async-start | bytes 2621440 | tf_op jit(solution)/shard_map/all_gather | solution.py:115
  10.6 161.5 %all-gather.20.cloned.1.call-start = ((), (), s32[]{:S(2)}) async-start(), calls=%async_computation.8 | async-start | bytes 5242880 | tf_op jit(solution)/shard_map/all_gather | solution.py:115
  36.9 94.3 %copy-start.25 = (f32[1024]{0:T(1024)}, f32[1024]{0:T(1024)S(1)}, u32[]{:S(2)}) copy-start(f32[1024]{0:T(1024)S(1)} %convert_add_fusion.2) | copy-start | bytes 12292
  88.9 9.2 %copy-start.5 = (bf16[512,1024]{0,1:T(8,128)(2,1)}, bf16[512,1024]{0,1:T(8,128)(2,1)S(1)}, u32[]{:S(2)}) copy-start(bf16[512,1024]{0,1:T(8,128)(2,1)S(1)} %copy.73) | copy-start | bytes 3145732
  112.9 9.4 %copy-start.11 = (bf16[512,1024]{0,1:T(8,128)(2,1)}, bf16[512,1024]{0,1:T(8,128)(2,1)S(1)}, u32[]{:S(2)}) copy-start(bf16[512,1024]{0,1:T(8,128)(2,1)S(1)} %copy.71) | copy-start | bytes 3145732
  137.5 113.1 %reduce-scatter.4.cloned.1.call-start = ((), (), s32[]{:S(2)}) async-start(), calls=%async_computation.9 | async-start | bytes 5242880 | tf_op jit(solution)/shard_map/reduce_scatter | solution.py:118
  172.1 27.7 %copy-start.33 = (bf16[1024,1024]{1,0:T(8,128)(2,1)S(1)}, bf16[1024,1024]{1,0:T(8,128)(2,1)}, u32[]{:S(2)}) copy-start(bf16[1024,1024]{1,0:T(8,128)(2,1)} %param.31) | copy-start | bytes 6291460
  205.9 47.8 %copy-start.12 = (bf16[512,1024]{1,0:T(8,128)(2,1)S(1)}, bf16[512,1024]{1,0:T(8,128)(2,1)}, u32[]{:S(2)}) copy-start(bf16[512,1024]{1,0:T(8,128)(2,1)} %param.24) | copy-start | bytes 3145732
  205.9 87.9 %all-gather.22.cloned.1.call-start = ((), (), s32[]{:S(2)}) async-start(), calls=%async_computation.10 | async-start | bytes 5242880 | tf_op jit(solution)/shard_map/all_gather | solution.py:115
  259.2 100.6 %reduce-scatter.6.cloned.1.call-start = ((), (), s32[]{:S(2)}) async-start(), calls=%async_computation.11 | async-start | bytes 5242880 | tf_op jit(solution)/shard_map/reduce_scatter | solution.py:118
  315.1 180.0 %reduce-scatter.8.cloned.1.call-start = ((), (), s32[]{:S(2)}) async-start(), calls=%async_computation.12 | async-start | bytes 10485760 | tf_op jit(solution)/shard_map/reduce_scatter | solution.py:118
  381.6 12.0 %copy-start.6 = (bf16[512,1024]{0,1:T(8,128)(2,1)S(1)}, bf16[512,1024]{0,1:T(8,128)(2,1)}, u32[]{:S(2)}) copy-start(bf16[512,1024]{0,1:T(8,128)(2,1)} %copy-done.5) | copy-start | bytes 3145732
  395.2 12.6 %copy-start.14 = (bf16[16,64,512]{2,1,0:T(8,128)(2,1)}, bf16[16,64,512]{2,1,0:T(8,128)(2,1)S(1)}, u32[]{:S(2)}) copy-start(bf16[16,64,512]{2,1,0:T(8,128)(2,1)S(1)} %get-tuple-element.69) | copy-start | bytes 3145732
  397.8 11.3 %copy-start.17 = (bf16[16,64,512]{2,1,0:T(8,128)(2,1)}, bf16[16,64,512]{2,1,0:T(8,128)(2,1)S(1)}, u32[]{:S(2)}) copy-start(bf16[16,64,512]{2,1,0:T(8,128)(2,1)S(1)} %multiply_convert_fusion.2) | copy-start | bytes 3145732
  399.1 8.7 %copy-start.21 = (bf16[512,1024]{1,0:T(8,128)(2,1)S(1)}, bf16[512,1024]{1,0:T(8,128)(2,1)}, u32[]{:S(2)}) copy-start(bf16[512,1024]{1,0:T(8,128)(2,1)} %param.21) | copy-start | bytes 3145732
  399.1 8.7 %copy-start.26 = (f32[1024]{0:T(1024)S(1)}, f32[1024]{0:T(1024)}, u32[]{:S(2)}) copy-start(f32[1024]{0:T(1024)} %copy-done.25) | copy-start | bytes 12292
  423.6 292.6 %all-reduce.3.cloned.1.call-start = ((), (), s32[]{:S(2)}) async-start(), calls=%async_computation.13 | async-start | bytes 12582912 | tf_op jit(solution)/shard_map/psum | solution.py:199
  439.3 55.9 %copy-start.15 = (bf16[16,64,512]{2,1,0:T(8,128)(2,1)S(1)}, bf16[16,64,512]{2,1,0:T(8,128)(2,1)}, u32[]{:S(2)}) copy-start(bf16[16,64,512]{2,1,0:T(8,128)(2,1)} %copy-done.14) | copy-start | bytes 3145732
  (26 other events, 73.0 us)
Sparse Core Ops, SparseCore 0:
  9.6 25.2 all-gather.9
  36.5 22.5 all-gather.13
  60.6 22.5 all-gather.15
  84.6 22.5 all-gather.11
  108.6 22.5 all-gather.17
  137.6 34.4 all-gather.19
  206.0 44.5 reduce-scatter.3
  259.3 34.4 all-gather.21
  315.2 44.5 reduce-scatter.5
  423.7 71.3 reduce-scatter.7
  499.6 216.4 all-reduce.2
where the time goes:
time: 741 us; the launch traced here: 732 us
  waiting for transfers between devices  443 us (60%)
  matrix products  138 us (19%)
  blocking collectives  51.7 us (7%)
  other arithmetic  47.2 us (6%)
  local copies, waits for them, and re-layouts  35.2 us (5%)
  between operations  15.6 us (2%)
    psum x1, waiting for transfers between devices, local(): sum_attn = lax.psum(share, 'dp').astype(f32)  157 us
    reduce_scatter x3, waiting for transfers between devices, scatter_sum(): return lax.psum_scatter(a, 'seq', scatter_dimension=0, tiled=True)  145 us
    all_gather x7, waiting for transfers between devices, gather(): return lax.all_gather(a, 'seq', axis=0, tiled=True)  138 us
    dot_general x20, matrix products, mm(): return lax.dot_general(a, b, (dims, ((), ())), preferred_element_type=f32)  96.6 us
    all_gather x1, blocking collectives, local(): every = lax.all_gather(small, ('dp', 'seq'), axis=0)  51.7 us
  transfers between devices with their start and end apart: 11, of which 11 were waited for; matrix products, arithmetic and copies ran while one was open for 10% of the time, Pallas kernels for 0%

commit v1 on v0

--- a/solution.py
+++ b/solution.py
@@ -196,7 +196,7 @@
     group = w_out.shape[0]
     stacked = jnp.stack([t.astype(bf16).reshape(-1, group, width) for t in terms], axis=1)
     share = scatter_sum(stacked.reshape(-1, width))
-    sum_attn = lax.psum(share, "dp").astype(f32)
+    sum_attn = jax.lax.all_gather(share, axis_name="dp").sum(axis=0).astype(f32)
     small = jnp.concatenate(
         [
             jnp.stack(

time: 741 us -> 913 us (1.23)
  waiting for transfers between devices: 443 us -> 612 us
  other arithmetic: 47.2 us -> 58 us
    all_gather x0 -> x1, waiting for transfers between devices: none -> 166 us  [local(): sum_attn = jax.lax.all_gather(share, axis_name='dp').sum(axis=0).astype(f32)]
    reduce_sum x0 -> x1, other arithmetic: none -> 10.8 us  [local(): sum_attn = jax.lax.all_gather(share, axis_name='dp').sum(axis=0).astype(f32)]
  transfers between devices with their start and end apart: 11 -> 12, of which waited for: 11 -> 12; matrix products, arithmetic and copies ran while one was open for 10% -> 9% of each run, Pallas kernels for 0% -> 0%
where the time goes in v1:
time: 913 us; the launch traced here: 904 us
  waiting for transfers between devices  612 us (67%)
  matrix products  137 us (15%)
  other arithmetic  58 us (6%)
  blocking collectives  49 us (5%)
  local copies, waits for them, and re-layouts  30.8 us (3%)
  between operations  15.9 us (2%)
    all_gather x1, waiting for transfers between devices, local(): sum_attn = jax.lax.all_gather(share, axis_name='dp').sum(axis=0).astype(f32)  166 us
    psum x1, waiting for transfers between devices, local(): lax.psum(jnp.concatenate([term_in, term_down], axis=0), 'dp').astype(f32)  161 us
    reduce_scatter x3, waiting for transfers between devices, scatter_sum(): return lax.psum_scatter(a, 'seq', scatter_dimension=0, tiled=True)  144 us
    all_gather x7, waiting for transfers between devices, gather(): return lax.all_gather(a, 'seq', axis=0, tiled=True)  138 us
    dot_general x20, matrix products, mm(): return lax.dot_general(a, b, (dims, ((), ())), preferred_element_type=f32)  94.9 us
    all_gather x1, blocking collectives, local(): every = lax.all_gather(small, ('dp', 'seq'), axis=0)  49 us
  transfers between devices with their start and end apart: 12, of which 12 were waited for; matrix products, arithmetic and copies ran while one was open for 9% of the time, Pallas kernels for 0%

profile of v1, /device:TPU:0, one launch (start us, length us, event | category | flops | bytes accessed | tf_op | source)
XLA Modules:
  0.0 904.0 jit_solution(4009528641068321788)
XLA Ops:
  16.0 18.9 %all-gather.12.cloned.1.call-done = bf16[1024,1024]{1,0:T(8,128)(2,1)} async-done(((bf16[256,1024]{1,0:T(8,128)(2,1)}), bf16[1024,1024]{1,0:T(8,128)(2,1)}) %all-gather.12.cloned.1.call-update) | async-done | bytes 2097168 | tf_op jit(solution)/shard_map/all_gather | solution.py:115
  36.9 22.1 %all-gather.16.cloned.1.call-done = bf16[1024,1024]{1,0:T(8,128)(2,1)} async-done(((bf16[256,1024]{1,0:T(8,128)(2,1)}), bf16[1024,1024]{1,0:T(8,128)(2,1)}) %all-gather.16.cloned.1.call-update) | async-done | bytes 2097168 | tf_op jit(solution)/shard_map/all_gather | solution.py:115
  63.6 19.7 %all-gather.18.cloned.1.call-done = bf16[1024,1024]{1,0:T(8,128)(2,1)} async-done(((bf16[256,1024]{1,0:T(8,128)(2,1)}), bf16[1024,1024]{1,0:T(8,128)(2,1)}) %all-gather.18.cloned.1.call-update) | async-done | bytes 2097168 | tf_op jit(solution)/shard_map/all_gather | solution.py:115
  88.9 9.2 %fusion.46 = (f32[16,512]{1,0:T(8,128)S(1)}, f32[16,512,512]{1,2,0:T(8,128)}) fusion(bf16[512,16,64]{0,2,1:T(8,128)(2,1)} %bitcast.99, bf16[512,16,64]{0,2,1:T(8,128)(2,1)S(1)} %bitcast.97, pred[512]{0:T(512)(128)(4,1)S(1)} %iota_compare_fusion), kind=kOutput, calls=%fused_computation.107 | convolution fusion | flops 549445632 | bytes 18907648 | tf_op jit(solution)/shard_map/qhd,khd->hqk/dot_general | solution.py:27
  98.1 9.2 %all-gather.14.cloned.1.call-done = bf16[1024,1024]{1,0:T(8,128)(2,1)} async-done(((bf16[256,1024]{1,0:T(8,128)(2,1)}), bf16[1024,1024]{1,0:T(8,128)(2,1)}) %all-gather.14.cloned.1.call-update) | async-done | bytes 2097168 | tf_op jit(solution)/shard_map/all_gather | solution.py:115
  112.9 9.4 %fusion = f32[16,512]{1,0:T(8,128)S(1)} fusion(f32[16,512,512]{1,2,0:T(8,128)} %get-tuple-element.59, f32[16,512]{1,0:T(8,128)S(1)} %get-tuple-element.58), kind=kLoop, calls=%fused_computation.6 | loop fusion | flops 8380416 | bytes 16842752 | tf_op jit(solution)/shard_map/reduce_sum | solution.py:37
  122.2 8.5 fusion.16
  138.5 33.7 %all-gather.22.cloned.1.call-done = bf16[2048,1024]{1,0:T(8,128)(2,1)} async-done(((bf16[512,1024]{1,0:T(8,128)(2,1)}), bf16[2048,1024]{1,0:T(8,128)(2,1)}) %all-gather.22.cloned.1.call-update) | async-done | bytes 4194320 | tf_op jit(solution)/shard_map/all_gather | solution.py:115
  172.1 25.6 %multiply_convert_fusion.1 = (bf16[2048,1024]{1,0:T(8,128)(2,1)S(1)}, f32[2048,1024]{1,0:T(8,128)}, f32[2048,1024]{1,0:T(8,128)}) fusion(f32[1024]{0:T(1024)S(1)} %dynamic-slice_convert_fusion, bf16[2048,1024]{1,0:T(8,128)(2,1)} %all-gather.22.cloned.1.call-done, bf16[1024,1024]{1,0:T(8,128)(2,1)S(1)} %copy-done), kind=kOutput, calls=%fused_computation.14 | convolution fusion | flops 4433379328 | bytes 27267072 | tf_op jit(solution)/shard_map/dot_general | solution.py:112
  199.8 6.0 convolution_convert_fusion.1
  206.5 44.0 %reduce-scatter.4.cloned.1.call-done = bf16[512,1024]{1,0:T(8,128)(2,1)} async-done(((bf16[2048,1024]{1,0:T(8,128)(2,1)}), bf16[512,1024]{1,0:T(8,128)(2,1)}) %reduce-scatter.4.cloned.1.call-update) | async-done | bytes 1048592 | tf_op jit(solution)/shard_map/reduce_scatter | solution.py:118
  259.6 34.2 %all-gather.24.cloned.1.call-done = bf16[2048,1024]{1,0:T(8,128)(2,1)} async-done(((bf16[512,1024]{1,0:T(8,128)(2,1)}), bf16[2048,1024]{1,0:T(8,128)(2,1)}) %all-gather.24.cloned.1.call-update) | async-done | bytes 4194320 | tf_op jit(solution)/shard_map/all_gather | solution.py:115
  293.8 13.3 %fusion.34 = (bf16[1024]{0:T(1024)(128)(2,1)S(1)}, bf16[2048,1024]{1,0:T(8,128)(2,1)S(1)}) fusion(f32[2048,1024]{1,0:T(8,128)} %get-tuple-element.38, f32[2048,1024]{1,0:T(8,128)} %get-tuple-element.62, f32[1024]{0:T(1024)S(1)} %dynamic-slice_convert_fusion, bf16[2048,1024]{1,0:T(8,128)(2,1)} %all-gather.24.cloned.1.call-done, bf16[1024,1024]{1,0:T(8,128)(2,1)} %param.31), kind=kOutput, calls=%fused_computation.96 | convolution fusion | flops 4328520704 | bytes 27269120 | tf_op jit(solution)/shard_map/dot_general | solution.py:112
  315.1 44.7 %reduce-scatter.6.cloned.1.call-done = bf16[512,1024]{1,0:T(8,128)(2,1)} async-done(((bf16[2048,1024]{1,0:T(8,128)(2,1)}), bf16[512,1024]{1,0:T(8,128)(2,1)}) %reduce-scatter.6.cloned.1.call-update) | async-done | bytes 1048592 | tf_op jit(solution)/shard_map/reduce_scatter | solution.py:118
  370.1 11.4 %multiply_reduce_fusion = (f32[16,512]{1,0:T(8,128)S(1)}, f32[16,512,512]{1,2,0:T(8,128)}) fusion(f32[16,512,512]{1,2,0:T(8,128)} %get-tuple-element.59, f32[16,512]{1,0:T(8,128)S(1)} %log_add_fusion, bf16[512,16,64]{0,2,1:T(8,128)(2,1)S(1)} %bitcast.101, bf16[512,16,64]{0,2,1:T(8,128)(2,1)} %bitcast.104), kind=kOutput, calls=%fused_computation.1 | convolution fusion | flops 549445632 | bytes 35717120 | tf_op jit(solution)/shard_map/qhd,khd->hqk/dot_general | solution.py:53
  381.5 12.0 %multiply_convert_fusion = bf16[16,512,512]{1,2,0:T(8,128)(2,1)S(1)} fusion(f32[16,512,512]{1,2,0:T(8,128)} %get-tuple-element.64, f32[16,512,512]{1,2,0:T(8,128)} %get-tuple-element.59, f32[16,512]{1,0:T(8,128)S(1)} %get-tuple-element.63, f32[16,512]{1,0:T(8,128)S(1)} %log_add_fusion), kind=kLoop, calls=%fused_computation | loop fusion | flops 16777216 | bytes 42008576 | tf_op jit(solution)/shard_map/convert_element_type | solution.py:57
  397.7 9.0 bitcast_reduce_fusion
  416.5 8.2 convolution_convert_fusion.2
  432.0 55.7 %reduce-scatter.8.cloned.1.call-done = bf16[1024,1024]{1,0:T(8,128)(2,1)} async-done(((bf16[4096,1024]{1,0:T(8,128)(2,1)}), bf16[1024,1024]{1,0:T(8,128)(2,1)}) %reduce-scatter.8.cloned.1.call-update) | async-done | bytes 2097168 | tf_op jit(solution)/shard_map/reduce_scatter | solution.py:118
  487.8 160.6 %all-reduce.2.cloned.1.call-done = bf16[2048,1024]{1,0:T(8,128)(2,1)} async-done(((bf16[2048,1024]{1,0:T(8,128)(2,1)}), bf16[2048,1024]{1,0:T(8,128)(2,1)}) %all-reduce.2.cloned.1.call-update) | async-done | bytes 4194320 | tf_op jit(solution)/shard_map/psum | solution.py:170
  648.4 6.8 fusion.41
  663.8 49.0 %all-gather.2 = bf16[32,11,1024]{2,1,0:T(8,128)(2,1)S(1)} all-gather(bf16[1,11,1024]{2,1,0:T(8,128)(2,1)S(1)} %bitcast.117), channel_id=3, replica_groups=mesh['dp'=8,'seq'=4] {'dp','seq'}, dimensions={0}, use_global_device_ids=true | all-gather | bytes 743424 | tf_op jit(solution)/shard_map/all_gather | solution.py:220
  716.7 165.5 %all-gather.26.cloned.1.call-done = bf16[8192,1024]{1,0:T(8,128)(2,1)} async-done(((bf16[1024,1024]{1,0:T(8,128)(2,1)}), bf16[8192,1024]{1,0:T(8,128)(2,1)}) %all-gather.26.cloned.1.call-update) | async-done | bytes 16777232 | tf_op jit(solution)/shard_map/all_gather | solution.py:199
  882.2 10.8 %reduce_sum.264 = bf16[1024,1024]{1,0:T(8,128)(2,1)} reduce(bf16[8,1024,1024]{2,1,0:T(8,128)(2,1)} %bitcast.96, bf16[]{:T(256)} %constant.103.clone.1), dimensions={0}, to_apply=%region_14.15 | reduce | flops 7340032 | bytes 18874370 | tf_op jit(solution)/shard_map/reduce_sum | solution.py:199
  (179 shorter events, 100.8 us)
Async XLA Ops:
  7.2 164.9 %copy-start = (bf16[1024,1024]{1,0:T(8,128)(2,1)S(1)}, bf16[1024,1024]{1,0:T(8,128)(2,1)}, u32[]{:S(2)}) copy-start(bf16[1024,1024]{1,0:T(8,128)(2,1)} %param.30) | copy-start | bytes 6291460
  7.2 29.7 %copy-start.27 = (bf16[1024]{0:T(1024)(128)(2,1)S(1)}, bf16[1024]{0:T(1024)(128)(2,1)}, u32[]{:S(2)}) copy-start(bf16[1024]{0:T(1024)(128)(2,1)} %param.35) | copy-start | bytes 6148
  7.2 27.7 %all-gather.12.cloned.1.call-start = ((), (), s32[]{:S(2)}) async-start(), calls=%async_computation.3 | async-start | bytes 2621440 | tf_op jit(solution)/shard_map/all_gather | solution.py:115
  7.9 51.1 %all-gather.16.cloned.1.call-start = ((), (), s32[]{:S(2)}) async-start(), calls=%async_computation.5 | async-start | bytes 2621440 | tf_op jit(solution)/shard_map/all_gather | solution.py:115
  8.7 74.5 %all-gather.18.cloned.1.call-start = ((), (), s32[]{:S(2)}) async-start(), calls=%async_computation.6 | async-start | bytes 2621440 | tf_op jit(solution)/shard_map/all_gather | solution.py:115
  9.4 97.8 %all-gather.14.cloned.1.call-start = ((), (), s32[]{:S(2)}) async-start(), calls=%async_computation.4 | async-start | bytes 2621440 | tf_op jit(solution)/shard_map/all_gather | solution.py:115
  10.0 121.2 %all-gather.20.cloned.1.call-start = ((), (), s32[]{:S(2)}) async-start(), calls=%async_computation.7 | async-start | bytes 2621440 | tf_op jit(solution)/shard_map/all_gather | solution.py:115
  10.6 161.5 %all-gather.22.cloned.1.call-start = ((), (), s32[]{:S(2)}) async-start(), calls=%async_computation.8 | async-start | bytes 5242880 | tf_op jit(solution)/shard_map/all_gather | solution.py:115
  36.9 94.3 %copy-start.24 = (f32[1024]{0:T(1024)}, f32[1024]{0:T(1024)S(1)}, u32[]{:S(2)}) copy-start(f32[1024]{0:T(1024)S(1)} %convert_add_fusion.2) | copy-start | bytes 12292
  88.9 9.2 %copy-start.5 = (bf16[512,1024]{0,1:T(8,128)(2,1)}, bf16[512,1024]{0,1:T(8,128)(2,1)S(1)}, u32[]{:S(2)}) copy-start(bf16[512,1024]{0,1:T(8,128)(2,1)S(1)} %copy.78) | copy-start | bytes 3145732
  112.9 9.4 %copy-start.10 = (bf16[512,1024]{0,1:T(8,128)(2,1)}, bf16[512,1024]{0,1:T(8,128)(2,1)S(1)}, u32[]{:S(2)}) copy-start(bf16[512,1024]{0,1:T(8,128)(2,1)S(1)} %copy.76) | copy-start | bytes 3145732
  137.5 113.1 %reduce-scatter.4.cloned.1.call-start = ((), (), s32[]{:S(2)}) async-start(), calls=%async_computation.9 | async-start | bytes 5242880 | tf_op jit(solution)/shard_map/reduce_scatter | solution.py:118
  172.1 27.7 %copy-start.32 = (bf16[1024,1024]{1,0:T(8,128)(2,1)S(1)}, bf16[1024,1024]{1,0:T(8,128)(2,1)}, u32[]{:S(2)}) copy-start(bf16[1024,1024]{1,0:T(8,128)(2,1)} %param.31) | copy-start | bytes 6291460
  205.8 47.8 %copy-start.11 = (bf16[512,1024]{1,0:T(8,128)(2,1)S(1)}, bf16[512,1024]{1,0:T(8,128)(2,1)}, u32[]{:S(2)}) copy-start(bf16[512,1024]{1,0:T(8,128)(2,1)} %param.24) | copy-start | bytes 3145732
  205.9 87.9 %all-gather.24.cloned.1.call-start = ((), (), s32[]{:S(2)}) async-start(), calls=%async_computation.10 | async-start | bytes 5242880 | tf_op jit(solution)/shard_map/all_gather | solution.py:115
  259.2 100.6 %reduce-scatter.6.cloned.1.call-start = ((), (), s32[]{:S(2)}) async-start(), calls=%async_computation.11 | async-start | bytes 5242880 | tf_op jit(solution)/shard_map/reduce_scatter | solution.py:118
  315.0 172.7 %reduce-scatter.8.cloned.1.call-start = ((), (), s32[]{:S(2)}) async-start(), calls=%async_computation.12 | async-start | bytes 10485760 | tf_op jit(solution)/shard_map/reduce_scatter | solution.py:118
  381.5 12.0 %copy-start.6 = (bf16[512,1024]{0,1:T(8,128)(2,1)S(1)}, bf16[512,1024]{0,1:T(8,128)(2,1)}, u32[]{:S(2)}) copy-start(bf16[512,1024]{0,1:T(8,128)(2,1)} %copy-done.5) | copy-start | bytes 3145732
  395.1 12.9 %copy-start.13 = (bf16[16,64,512]{2,1,0:T(8,128)(2,1)}, bf16[16,64,512]{2,1,0:T(8,128)(2,1)S(1)}, u32[]{:S(2)}) copy-start(bf16[16,64,512]{2,1,0:T(8,128)(2,1)S(1)} %get-tuple-element.67) | copy-start | bytes 3145732
  397.7 12.0 %copy-start.16 = (bf16[16,64,512]{2,1,0:T(8,128)(2,1)}, bf16[16,64,512]{2,1,0:T(8,128)(2,1)S(1)}, u32[]{:S(2)}) copy-start(bf16[16,64,512]{2,1,0:T(8,128)(2,1)S(1)} %multiply_convert_fusion.2) | copy-start | bytes 3145732
  397.7 9.0 copy-start.19
  416.2 232.2 %all-reduce.2.cloned.1.call-start = ((), (), s32[]{:S(2)}) async-start(), calls=%async_computation.13 | async-start | bytes 8388608 | tf_op jit(solution)/shard_map/psum | solution.py:170
  431.9 450.3 %all-gather.26.cloned.1.call-start = ((), (), s32[]{:S(2)}) async-start(), calls=%async_computation.14 | async-start | bytes 18874368 | tf_op jit(solution)/shard_map/all_gather | solution.py:199
  487.8 167.4 %copy-start.14 = (bf16[16,64,512]{2,1,0:T(8,128)(2,1)S(1)}, bf16[16,64,512]{2,1,0:T(8,128)(2,1)}, u32[]{:S(2)}) copy-start(bf16[16,64,512]{2,1,0:T(8,128)(2,1)} %copy-done.13) | copy-start | bytes 3145732
  (27 other events, 80.7 us)
Sparse Core Ops, SparseCore 0:
  9.6 25.2 all-gather.11
  36.5 22.5 all-gather.15
  60.6 22.5 all-gather.17
  84.6 22.5 all-gather.13
  108.6 22.5 all-gather.19
  137.6 34.4 all-gather.21
  206.0 44.5 reduce-scatter.3
  259.3 34.4 all-gather.23
  315.1 44.5 reduce-scatter.5
  416.3 71.3 reduce-scatter.7
  492.0 156.3 all-reduce.1
  650.4 231.7 all-gather.25
